TPU v7x, 128 devices: a whole 4x4x4 slice. The times are simulated.
128 devices in a mesh: blk: 16 (over x_lo, y, core), feat: 8 (over z, x_hi).
Axes of the slice: x: 4 (x_hi: 2, x_lo: 2; x = x_hi * 2 + x_lo), y: 4, z: 4, core: 2. Of those that a mesh axis runs over, the one named last changes fastest.
Arguments:
- features: bfloat16 [256, 32768], P('feat', 'blk'), may hold values from -6 to 6
- adj_tiles: bfloat16 [16, 8, 16, 48, 128, 128], P('blk', 'feat'), may hold values from -0.02734375 to 0.02734375
- tile_rows: int32 [16, 8, 16, 48], P('blk', 'feat'), may hold values from 0 to 15
- tile_cols: int32 [16, 8, 16, 48], P('blk', 'feat'), may hold values from 0 to 15
- counts: int32 [16, 8, 16], P('blk', 'feat'), may hold values from 1 to 48, as said below
- weight: bfloat16 [256, 256], replicated, may hold values from -0.375 to 0.375
- cotangent: bfloat16 [256, 32768], P(None, ('blk', 'feat')), may hold values from -6 to 6
Outputs:
- activated: bfloat16 [256, 32768], P(None, ('blk', 'feat'))
- weight_grad: float32 [256, 256], P('feat')
Inputs may be any that keep to these rules, and one draw needn't show every extreme that they name: Only the first counts slots of a partition, group and source partition are live; the slots a partition takes from its own nodes are all live in every group.
All inputs are finite; a program needn't handle non-finite values.
Results may differ from a plain program's by a relative error of at most 0.02.
Values may be sent and summed in bfloat16 or wider, within the bound.
A program may use at most 320 MiB of HBM per device.

v0:
```python
import math

import jax
import jax.numpy as jnp
from jax import lax
from jax.sharding import PartitionSpec as P


def tile_terms(slot_tiles, gathered, rows_here, live_mask, row_tiles):
    products = jnp.einsum("kij,fkj->fki", slot_tiles, gathered, preferred_element_type=jnp.float32)
    tile_range = jnp.arange(row_tiles, dtype=jnp.int32)
    placing = ((rows_here[:, None] == tile_range[None, :]) & live_mask[:, None]).astype(
        jnp.bfloat16
    )
    high_part = lax.optimization_barrier(products.astype(jnp.bfloat16))
    low_part = (products - high_part.astype(jnp.float32)).astype(jnp.bfloat16)
    summed = jnp.einsum("fki,kr->fri", high_part, placing, preferred_element_type=jnp.float32)
    summed = summed + jnp.einsum(
        "fki,kr->fri", low_part, placing, preferred_element_type=jnp.float32
    )
    return summed.reshape(products.shape[0], row_tiles * products.shape[2])


def source_term(col_panel, job, source, accum, row_tiles):
    job_tiles, job_rows, job_cols, job_counts = job
    slot_tiles = lax.dynamic_index_in_dim(job_tiles, source, 0, False)
    slot_rows = lax.dynamic_index_in_dim(job_rows, source, 0, False)
    slot_cols = lax.dynamic_index_in_dim(job_cols, source, 0, False)
    slot_count = lax.dynamic_index_in_dim(job_counts, source, 0, False)
    slot_cap = slot_tiles.shape[0]
    gathered = jnp.take(col_panel, slot_cols, axis=1)
    live_mask = jnp.arange(slot_cap, dtype=jnp.int32) < slot_count
    return accum + tile_terms(slot_tiles, gathered, slot_rows, live_mask, row_tiles)


def shards(features, adj_tiles, tile_rows, tile_cols, counts, weight, cotangent):
    blocks = lax.axis_size("blk")
    groups = lax.axis_size("feat")
    group_width = features.shape[0]
    feat_width = group_width * groups
    rows_here = features.shape[1]
    tile_size = adj_tiles.shape[-1]
    row_tiles = rows_here // tile_size
    slot_cap = adj_tiles.shape[3]
    local_tiles = adj_tiles.reshape(blocks, slot_cap, tile_size, tile_size)
    local_rows = tile_rows.reshape(blocks, slot_cap)
    local_cols = tile_cols.reshape(blocks, slot_cap)
    local_counts = counts.reshape(blocks)
    jobs = [(local_tiles, local_rows, local_cols, local_counts)]
    full_rows = lax.all_gather(features, "feat", axis=0, tiled=True)
    start_sums = tuple((jnp.zeros((feat_width, rows_here), jnp.float32) for job in jobs))
    shard_piece = lax.all_gather(full_rows, "blk", axis=1, tiled=True)

    def add_source(offset, inner):
        col_panel = lax.dynamic_slice_in_dim(shard_piece, offset * rows_here, rows_here, 1)
        col_panel = col_panel.reshape(feat_width, row_tiles, tile_size)
        return tuple(
            (
                source_term(col_panel, job, offset, total, row_tiles)
                for job, total in zip(jobs, inner)
            )
        )

    sums_all = lax.fori_loop(0, shard_piece.shape[1] // rows_here, add_source, start_sums)
    partial_value = sums_all[0]
    aggregated = lax.psum_scatter(
        partial_value.astype(jnp.bfloat16), "feat", scatter_dimension=1, tiled=True
    )
    preact = jnp.dot(weight, aggregated, preferred_element_type=jnp.float32)
    sigmoid_z = jax.nn.sigmoid(preact)
    activated = (preact * sigmoid_z).astype(jnp.bfloat16)
    slope = (cotangent.astype(jnp.float32) * sigmoid_z * (1.0 + preact * (1.0 - sigmoid_z))).astype(
        jnp.bfloat16
    )
    grad_scale = 1.0 / math.sqrt(blocks * rows_here)
    local_grad = (
        lax.dot_general(
            slope, aggregated, (((1,), (1,)), ((), ())), preferred_element_type=jnp.float32
        )
        * grad_scale
    )
    grad_whole = lax.psum(local_grad, ("blk", "feat"))
    grad_share = feat_width // groups
    weight_grad = lax.dynamic_slice_in_dim(
        grad_whole, lax.axis_index("feat") * grad_share, grad_share, 0
    )
    return (activated, weight_grad)


def solution(mesh):
    in_specs = (
        P("feat", "blk"),
        P("blk", "feat", None, None, None, None),
        P("blk", "feat", None, None),
        P("blk", "feat", None, None),
        P("blk", "feat", None),
        P(),
        P(None, ("blk", "feat")),
    )
    out_specs = (P(None, ("blk", "feat")), P("feat", None))
    return jax.shard_map(shards, mesh=mesh, in_specs=in_specs, out_specs=out_specs, check_vma=False)
```

profile of v0, /device:TPU:1, one launch (start us, length us, event | category | flops | bytes accessed | tf_op | source)
XLA Modules:
  0.0 712.7 jit_solution(4243127706743724954)
XLA Ops:
  8.0 50.9 %all-gather.3.cloned.1.call-done = bf16[256,2048]{1,0:T(8,128)(2,1)} async-done(((bf16[32,2048]{1,0:T(8,128)(2,1)}), bf16[256,2048]{1,0:T(8,128)(2,1)}) %all-gather.3.cloned.1.call-update) | async-done | bytes 1048592 | tf_op jit(solution)/shard_map/all_gather | solution.py:50
  58.9 93.6 %all-gather.5.cloned.1.call-done = bf16[256,32768]{1,0:T(8,128)(2,1)} async-done(((bf16[256,2048]{1,0:T(8,128)(2,1)}), bf16[256,32768]{1,0:T(8,128)(2,1)}) %all-gather.5.cloned.1.call-update) | async-done | bytes 16777232 | tf_op jit(solution)/shard_map/all_gather | solution.py:52
  152.5 331.1 %while.14 = (s32[]{:T(128)}, f32[256,2048]{1,0:T(8,128)}, s32[16,48]{1,0:T(8,128)}, s32[16]{0:T(128)}, s32[16,48]{1,0:T(8,128)}, /*index=5*/bf16[256,32768]{1,0:...) while((s32[]{:T(128)}, f32[256,2048]{1,0:T(8,128)}, ...), condition=%wide.region_1.2_spmd.clone, body=%wide.region_0.1_spmd.clone.sunk | while | flops 512758272 | bytes 58203024 | solution.py:64
  155.7 2.7 gather_fusion
  159.0 3.4 bitcast_convert_fusion.2
  174.9 2.7 gather_fusion
  178.3 3.4 bitcast_convert_fusion.2
  188.4 4.0 bitcast_add_fusion.2
  199.0 3.4 bitcast_convert_fusion.2
  209.2 4.0 bitcast_add_fusion.2
  216.5 2.7 gather_fusion
  219.8 3.4 bitcast_convert_fusion.2
  230.0 4.0 bitcast_add_fusion.2
  240.6 3.4 bitcast_convert_fusion.2
  250.8 4.0 bitcast_add_fusion.2
  258.0 2.7 gather_fusion
  261.4 3.4 bitcast_convert_fusion.2
  271.6 4.0 bitcast_add_fusion.2
  278.8 2.7 gather_fusion
  282.2 3.4 bitcast_convert_fusion.2
  292.4 4.0 bitcast_add_fusion.2
  299.6 2.7 gather_fusion
  303.0 3.4 bitcast_convert_fusion.2
  313.2 4.0 bitcast_add_fusion.2
  320.4 2.7 gather_fusion
  323.8 3.4 bitcast_convert_fusion.2
  334.0 4.0 bitcast_add_fusion.2
  341.2 2.7 gather_fusion
  344.6 3.4 bitcast_convert_fusion.2
  354.8 4.0 bitcast_add_fusion.2
  362.0 2.7 gather_fusion
  365.4 3.4 bitcast_convert_fusion.2
  375.6 4.0 bitcast_add_fusion.2
  382.8 2.7 gather_fusion
  386.2 3.4 bitcast_convert_fusion.2
  396.4 4.0 bitcast_add_fusion.2
  403.6 2.7 gather_fusion
  407.0 3.4 bitcast_convert_fusion.2
  417.2 4.0 bitcast_add_fusion.2
  427.8 3.4 bitcast_convert_fusion.2
  437.9 4.0 bitcast_add_fusion.2
  448.5 3.4 bitcast_convert_fusion.2
  458.7 4.0 bitcast_add_fusion.2
  469.3 3.4 bitcast_convert_fusion.2
  479.5 4.0 bitcast_add_fusion.2
  483.5 2.8 convert_element_type.36
  486.5 70.5 %reduce-scatter.2.cloned.1.call-done = bf16[256,256]{1,0:T(8,128)(2,1)} async-done(((bf16[256,2048]{1,0:T(8,128)(2,1)}), bf16[256,256]{1,0:T(8,128)(2,1)}) %reduce-scatter.2.cloned.1.call-update) | async-done | bytes 131088 | tf_op jit(solution)/shard_map/reduce_scatter | solution.py:66
  560.9 144.0 %all-reduce.2.cloned.1.call-done = f32[256,256]{1,0:T(8,128)} async-done(((f32[256,256]{1,0:T(8,128)}), f32[256,256]{1,0:T(8,128)}) %all-reduce.2.cloned.1.call-update) | async-done | bytes 262160 | tf_op jit(solution)/shard_map/psum | solution.py:82
  (248 shorter events, 192.6 us)
Async XLA Ops:
  7.2 549.8 %copy-start = (bf16[256,256]{1,0:T(8,128)(2,1)S(1)}, bf16[256,256]{1,0:T(8,128)(2,1)}, u32[]{:S(2)}) copy-start(bf16[256,256]{1,0:T(8,128)(2,1)} %param.14) | copy-start | bytes 393220
  7.2 51.6 %all-gather.3.cloned.1.call-start = ((), (), s32[]{:S(2)}) async-start(), calls=%async_computation.1 | async-start | bytes 1179648 | tf_op jit(solution)/shard_map/all_gather | solution.py:50
  7.9 144.6 %all-gather.5.cloned.1.call-start = ((), (), s32[]{:S(2)}) async-start(), calls=%async_computation.2 | async-start | bytes 17825792 | tf_op jit(solution)/shard_map/all_gather | solution.py:52
  58.8 498.1 %reduce-scatter.2.cloned.1.call-start = ((), (), s32[]{:S(2)}) async-start(), calls=%async_computation.3 | async-start | bytes 1179648 | tf_op jit(solution)/shard_map/reduce_scatter | solution.py:66
  162.4 1.2 copy-start.2
  181.6 1.2 copy-start.2
  202.4 1.2 copy-start.2
  223.2 1.2 copy-start.2
  244.0 1.2 copy-start.2
  264.8 1.2 copy-start.2
  285.6 1.2 copy-start.2
  306.4 1.2 copy-start.2
  327.2 1.2 copy-start.2
  348.0 1.2 copy-start.2
  368.8 1.2 copy-start.2
  389.6 1.2 copy-start.2
  410.3 1.2 copy-start.2
  431.1 1.2 copy-start.2
  451.9 1.2 copy-start.2
  472.7 1.2 copy-start.2
  483.5 2.8 copy-start.1
  486.3 218.5 %all-reduce.2.cloned.1.call-start = ((), (), s32[]{:S(2)}) async-start(), calls=%async_computation.4 | async-start | bytes 524288 | tf_op jit(solution)/shard_map/psum | solution.py:82
Sparse Core Ops, SparseCore 0:
  10.4 48.4 all-gather.2
  60.5 91.9 all-gather.4
  486.4 70.4 reduce-scatter.1
  562.3 142.4 all-reduce.1
where the time goes:
time: 716 us; the launch traced here: 713 us
  waiting for transfers between devices  360 us (50%)
  other arithmetic  117 us (16%)
  matrix products  116 us (16%)
  local copies, waits for them, and re-layouts  105 us (15%)
  between operations  13.8 us (2%)
    psum x1, waiting for transfers between devices, shards(): grad_whole = lax.psum(local_grad, ('blk', 'feat'))  144 us
    all_gather x1, waiting for transfers between devices, shards(): shard_piece = lax.all_gather(full_rows, 'blk', axis=1, tiled=True)  93.6 us
    reduce_scatter x1, waiting for transfers between devices, shards(): lax.psum_scatter(partial_value.astype(jnp.bfloat16), 'feat', scatter_dime...  70.5 us
    add x16, other arithmetic, source_term(): accum + tile_terms(slot_tiles, gathered, slot_rows, live_mask, row_tiles)  62.7 us
    dot_general x16, matrix products, tile_terms(): jnp.einsum('kij,fkj->fki', slot_tiles, gathered, preferred_element_type=j...  54 us
    all_gather x1, waiting for transfers between devices, shards(): full_rows = lax.all_gather(features, 'feat', axis=0, tiled=True)  50.9 us
    gather x16, local copies, waits for them, and re-layouts, source_term(): gathered = jnp.take(col_panel, slot_cols, axis=1)  42.8 us
    dot_general x16, matrix products, tile_terms(): jnp.einsum('fki,kr->fri', high_part, placing, preferred_element_type=jnp....  30 us
  transfers between devices with their start and end apart: 4, of which 4 were waited for; matrix products, arithmetic and copies ran while one was open for 0% of the time, Pallas kernels for 0%

commit v1 on v0

v1 whole, which is shorter than its diff:
```python
import functools
import math

import jax
import jax.numpy as jnp
from jax import lax
from jax.experimental import pallas as pl
from jax.experimental.pallas import tpu as pltpu
from jax.sharding import PartitionSpec as P

MESH = pl.DeviceIdType.MESH
TILE = 128
ORDERS = (("x", "y", "z"), ("y", "z", "x"), ("z", "x", "y"))
COLUMNS = ((0, 3, 6), (6, 8, 11), (11, 14, 16))
MIB = 2**20


def place():
    blk = lax.axis_index("blk")
    feat = lax.axis_index("feat")
    return {
        "x": (feat % 2) * 2 + blk // 8,
        "y": (blk // 2) % 4,
        "z": feat // 2,
        "c": blk % 2,
    }


def device(at):
    return {
        "blk": ((at["x"] % 2) * 4 + at["y"]) * 2 + at["c"],
        "feat": at["z"] * 2 + at["x"] // 2,
    }


def moved(at, dim, by):
    return {**at, dim: (at[dim] + by) % (2 if dim == "c" else 4)}


class Sender:
    def __init__(self, send_sem, recv_sem):
        self.send_sem, self.recv_sem, self.used = send_sem, recv_sem, 0
        self.all = []

    def start(self, ref, to):
        i = self.used
        self.used += 1
        copy = pltpu.make_async_remote_copy(
            src_ref=ref,
            dst_ref=ref,
            send_sem=self.send_sem.at[i],
            recv_sem=self.recv_sem.at[i],
            device_id=device(to),
            device_id_type=MESH,
        )
        self.all.append(copy)
        copy.start()
        return copy


N_COPIES = 3 * 24


def gather_kernel(x_ref, full, own_sem, send_sem, recv_sem):
    me = place()
    sibling = moved(me, "c", 1)
    neighbours = [moved(me, d, by) for d in "xyz" for by in (1, 3)] + [sibling]

    def region(at, lo, hi):
        def index(value):
            if value is None:
                return slice(None)
            if isinstance(value, tuple):
                return slice(2 * value[1], 2 * value[1] + 2)
            return pl.ds(value, 1)

        x = at["x"]
        if x is None:
            x_lo, x_hi = slice(None), slice(None)
        elif isinstance(x, tuple):
            x_lo, x_hi = slice(None), pl.ds(x[1], 1)
        else:
            x_lo, x_hi = pl.ds(x % 2, 1), pl.ds(x // 2, 1)
        return full.at[
            x_lo, index(at["y"]), pl.ds(me["c"], 1), lo:hi, index(at["z"]), x_hi
        ]

    barrier = pltpu.get_barrier_semaphore()
    for other in neighbours:
        pl.semaphore_signal(barrier, inc=1, device_id=device(other), device_id_type=MESH)
    own = []
    for ct in range(16):
        own.append(
            pltpu.make_async_copy(
                x_ref.at[:, ct * TILE : (ct + 1) * TILE],
                full.at[me["x"] % 2, me["y"], me["c"], ct, me["z"], me["x"] // 2],
                own_sem.at[ct],
            )
        )
        own[-1].start()
    for copy in own:
        copy.wait()
    pl.semaphore_wait(barrier, len(neighbours))

    net = Sender(send_sem, recv_sem)
    passed = []
    state = [{} for _ in ORDERS]
    for (d1, d2, d3), (lo, mid, hi), st in zip(ORDERS, COLUMNS, state):
        st["a"] = net.start(region(me, lo, hi), moved(me, d1, 1))
        st["b"] = net.start(region(me, lo, hi), moved(me, d1, 3))
    for (d1, d2, d3), (lo, mid, hi), st in zip(ORDERS, COLUMNS, state):
        st["a"].wait_recv()
        st["ah"] = net.start(region(moved(me, d1, 3), lo, mid), moved(me, d1, 1))
        st["b"].wait_recv()
        st["bh"] = net.start(region(moved(me, d1, 1), mid, hi), moved(me, d1, 3))
    for stage in (2, 3):
        for (d1, d2, d3), (lo, mid, hi), st in zip(ORDERS, COLUMNS, state):
            inner, ring = (d1, d2) if stage == 2 else (d2, d3)
            held = {**me, d1: None}
            if stage == 3:
                held[d2] = None
            if stage == 2:
                st["ah"].wait_recv()
                st["bh"].wait_recv()
            else:
                for name in ("p1", "m0", "pf", "mf"):
                    st[name].wait_recv()
                passed.append(net.start(region(held, lo, hi), sibling))
            for name, by, half in (("p0", 1, 0), ("m1", 3, 1), ("p1", 1, 1), ("m0", 3, 0)):
                st[name] = net.start(
                    region({**held, inner: ("h", half)}, lo, hi), moved(me, ring, by)
                )
            st["held"], st["inner"], st["ring"] = held, inner, ring

        def came(st, by, half):
            return {**moved(st["held"], st["ring"], by), st["inner"]: ("h", half)}

        for (lo, mid, hi), st in zip(COLUMNS, state):
            st["p0"].wait_recv()
            st["pf"] = net.start(region(came(st, 3, 0), lo, hi), moved(me, st["ring"], 1))
            if stage == 3:
                passed.append(net.start(region(came(st, 3, 0), lo, hi), sibling))
            st["m1"].wait_recv()
            st["mf"] = net.start(region(came(st, 1, 1), lo, hi), moved(me, st["ring"], 3))
            if stage == 3:
                passed.append(net.start(region(came(st, 1, 1), lo, hi), sibling))
    for name, by, half in (("p1", 3, 1), ("m0", 1, 0), ("pf", 2, 0), ("mf", 2, 1)):
        for (lo, mid, hi), st in zip(COLUMNS, state):
            st[name].wait_recv()
            passed.append(net.start(region(came(st, by, half), lo, hi), sibling))
    for copy in passed:
        copy.wait_recv()
    for copy in net.all:
        copy.wait_send()


def gather(features):
    return pl.pallas_call(
        gather_kernel,
        out_shape=jax.ShapeDtypeStruct((2, 4, 2, 16, 4, 2, 32, TILE), jnp.bfloat16),
        in_specs=[pl.BlockSpec(memory_space=pl.ANY)],
        out_specs=pl.BlockSpec(memory_space=pl.ANY),
        scratch_shapes=[
            pltpu.SemaphoreType.DMA((16,)),
            pltpu.SemaphoreType.DMA((N_COPIES,)),
            pltpu.SemaphoreType.DMA((N_COPIES,)),
        ],
        compiler_params=pltpu.CompilerParams(collective_id=0, has_side_effects=True),
        name="gather",
    )(features)


CHUNK = 16


def aggregate_kernel(
    rows_ref, cols_ref, counts_ref, full_hbm, tiles_hbm, out_ref, full, tiles, total, fsem, tsem
):
    sources, slots = tiles_hbm.shape[:2]

    def full_copy(s):
        return pltpu.make_async_copy(full_hbm.at[s], full.at[s], fsem.at[s])

    def chunk_copy(s, c):
        part = pl.ds(c * CHUNK, CHUNK)
        return pltpu.make_async_copy(
            tiles_hbm.at[s, part], tiles.at[s, part], tsem.at[s, c]
        )

    def over_chunks(s, act):
        for c in range(slots // CHUNK):
            pl.when(counts_ref[s] > c * CHUNK)(lambda c=c: act(chunk_copy(s, c)))

    @pl.loop(0, sources)
    def _(s):
        full_copy(s).start()
        over_chunks(s, lambda copy: copy.start())

    total[...] = jnp.zeros_like(total)

    @pl.loop(0, sources)
    def _(s):
        full_copy(s).wait()
        over_chunks(s, lambda copy: copy.wait())

        @pl.loop(0, counts_ref[s])
        def _(k):
            at = pl.ds(pl.multiple_of(rows_ref[s, k] * TILE, TILE), TILE)
            total[at, :] += lax.dot_general(
                tiles[s, k],
                full[s, cols_ref[s, k]],
                (((1,), (1,)), ((), ())),
                preferred_element_type=jnp.float32,
            )

    out_ref[...] = total[...].astype(out_ref.dtype)


def aggregate(rows, cols, counts, full, tiles):
    sources, slots = tiles.shape[:2]
    smem = pl.BlockSpec(memory_space=pltpu.SMEM)
    hbm = pl.BlockSpec(memory_space=pl.ANY)
    return pl.pallas_call(
        aggregate_kernel,
        out_shape=jax.ShapeDtypeStruct((2048, 256), jnp.bfloat16),
        in_specs=[smem, smem, smem, hbm, hbm],
        out_specs=pl.BlockSpec(memory_space=pltpu.VMEM),
        scratch_shapes=[
            pltpu.VMEM(full.shape, jnp.bfloat16),
            pltpu.VMEM(tiles.shape, jnp.bfloat16),
            pltpu.VMEM((2048, 256), jnp.float32),
            pltpu.SemaphoreType.DMA((sources,)),
            pltpu.SemaphoreType.DMA((sources, slots // CHUNK)),
        ],
        compiler_params=pltpu.CompilerParams(vmem_limit_bytes=58 * MIB),
        name="aggregate",
    )(rows, cols, counts, full, tiles)


def tail_kernel(
    part, weight, cotangent, act_ref, grad_ref,
    held, terms, terms_in, mine, mine_in, done,
    psem, pin, tsem, tin, msem, min_, dsem, din,
):
    blk, feat = lax.axis_index("blk"), lax.axis_index("feat")
    chip, core = blk // 2, blk % 2
    barrier = pltpu.get_barrier_semaphore()
    for i in range(1, 8):
        pl.semaphore_signal(
            barrier, inc=1, device_id={"feat": (feat + i) % 8}, device_id_type=MESH
        )
    for i in range(1, 16):
        pl.semaphore_signal(
            barrier, inc=1, device_id={"blk": (blk + i) % 16}, device_id_type=MESH
        )
    pl.semaphore_wait(barrier, 22)

    def remote(src, dst, send, recv, to):
        copy = pltpu.make_async_remote_copy(
            src_ref=src, dst_ref=dst, send_sem=send, recv_sem=recv,
            device_id=to, device_id_type=MESH,
        )
        copy.start()
        return copy

    sent = []
    for i in range(1, 8):
        to = (feat + i) % 8
        sent.append(
            remote(part.at[to], held.at[i - 1], psem.at[i - 1], pin.at[i - 1], {"feat": to})
        )
    summed = part[feat].astype(jnp.float32)
    for i in range(7):
        sent[i].wait_recv()
        summed = summed + held[i].astype(jnp.float32)
    nodes = summed.astype(jnp.bfloat16)
    preact = lax.dot_general(
        weight[...], nodes, (((1,), (1,)), ((), ())), preferred_element_type=jnp.float32
    )
    sigmoid = jax.nn.sigmoid(preact)
    act_ref[...] = (preact * sigmoid).astype(jnp.bfloat16)
    slope = cotangent[...].astype(jnp.float32) * sigmoid * (1.0 + preact * (1.0 - sigmoid))
    local = jnp.dot(slope.astype(jnp.bfloat16), nodes, preferred_element_type=jnp.float32)
    terms[...] = local.reshape(terms.shape)
    sent_terms = []
    for i in range(1, 8):
        to = (feat + i) % 8
        sent_terms.append(
            remote(terms.at[to], terms_in.at[i - 1], tsem.at[i - 1], tin.at[i - 1], {"feat": to})
        )
    share = terms[feat]
    for i in range(7):
        sent_terms[i].wait_recv()
        share = share + terms_in[i]
    for q in range(8):
        r, c = q // 2 * 8, q % 2 * 128
        mine[q] = share[r : r + 8, c : c + 128]
    sent_mine = []
    for i in range(1, 16):
        to = (blk + i) % 16
        sent_mine.append(
            remote(mine.at[to // 2], mine_in.at[i - 1], msem.at[i - 1], min_.at[i - 1], {"blk": to})
        )
    piece = mine[chip]
    for i in range(15):
        sent_mine[i].wait_recv()
        piece = piece + mine_in[i]
    done[chip] = piece * (1.0 / math.sqrt(32768))
    sent_done = []
    for i in range(1, 8):
        to = (chip + i) % 8 * 2 + core
        sent_done.append(
            remote(done.at[chip], done.at[chip], dsem.at[i - 1], din.at[i - 1], {"blk": to})
        )
    for copy in sent_done:
        copy.wait_recv()
    for q in range(8):
        r, c = q // 2 * 8, q % 2 * 128
        grad_ref[r : r + 8, c : c + 128] = done[q]
    for copy in sent + sent_terms + sent_mine + sent_done:
        copy.wait_send()


def tail(part, weight, cotangent):
    vmem = pl.BlockSpec(memory_space=pltpu.VMEM)
    dma = pltpu.SemaphoreType.DMA
    return pl.pallas_call(
        tail_kernel,
        out_shape=(
            jax.ShapeDtypeStruct((256, 256), jnp.bfloat16),
            jax.ShapeDtypeStruct((32, 256), jnp.float32),
        ),
        in_specs=[vmem] * 3,
        out_specs=(vmem, vmem),
        scratch_shapes=[
            pltpu.VMEM((7, 256, 256), jnp.bfloat16),
            pltpu.VMEM((8, 32, 256), jnp.float32),
            pltpu.VMEM((7, 32, 256), jnp.float32),
            pltpu.VMEM((8, 8, 128), jnp.float32),
            pltpu.VMEM((15, 8, 128), jnp.float32),
            pltpu.VMEM((8, 8, 128), jnp.float32),
            dma((7,)), dma((7,)), dma((7,)), dma((7,)),
            dma((15,)), dma((15,)), dma((7,)), dma((7,)),
        ],
        compiler_params=pltpu.CompilerParams(collective_id=1, has_side_effects=True),
        name="tail",
    )(part, weight, cotangent)


def shards(features, adj_tiles, tile_rows, tile_cols, counts, weight, cotangent):
    sources, slots = adj_tiles.shape[2:4]
    tiles = adj_tiles.reshape(sources, slots, TILE, TILE)
    full = gather(features).reshape(sources, 16, 256, TILE)
    part = aggregate(
        tile_rows.reshape(sources, slots),
        tile_cols.reshape(sources, slots),
        counts.reshape(sources),
        full,
        tiles,
    )
    return tail(part.reshape(8, 256, 256), weight, cotangent)


def solution(mesh):
    in_specs = (
        P("feat", "blk"),
        P("blk", "feat", None, None, None, None),
        P("blk", "feat", None, None),
        P("blk", "feat", None, None),
        P("blk", "feat", None),
        P(),
        P(None, ("blk", "feat")),
    )
    out_specs = (P(None, ("blk", "feat")), P("feat", None))
    return jax.shard_map(shards, mesh=mesh, in_specs=in_specs, out_specs=out_specs, check_vma=False)
```

time: 716 us -> 179 us (0.25)
  waiting for transfers between devices: 360 us -> 0 us
  Pallas kernels: 0 us -> 175 us
  other arithmetic: 117 us -> 0 us
  matrix products: 116 us -> 0 us
  local copies, waits for them, and re-layouts: 105 us -> 2.94 us
  between operations: 13.8 us -> 0.65 us
    pallas_call x0 -> x3, Pallas kernels: none -> 175 us  [the longest x1 76.6 us: aggregate(): pl.pallas_call(aggregate_kernel, out_shape=jax.ShapeDtypeStruct((2048, 25...]
    all_gather x2 -> x0, waiting for transfers between devices: 144 us -> none  [the longest x1 93.6 us: shards(): shard_piece = lax.all_gather(full_rows, 'blk', axis=1, tiled=True)]
    psum x1 -> x0, waiting for transfers between devices: 144 us -> none  [shards(): grad_whole = lax.psum(local_grad, ('blk', 'feat'))]
    dot_general x50 -> x0, matrix products: 116 us -> none  [the longest x16 54 us: tile_terms(): jnp.einsum('kij,fkj->fki', slot_tiles, gathered, preferred_element_type=j...]
    reduce_scatter x1 -> x0, waiting for transfers between devices: 70.5 us -> none  [shards(): lax.psum_scatter(partial_value.astype(jnp.bfloat16), 'feat', scatter_dime...]
    add x16 -> x0, other arithmetic: 62.7 us -> none  [source_term(): accum + tile_terms(slot_tiles, gathered, slot_rows, live_mask, row_tiles)]
    gather x16 -> x0, local copies, waits for them, and re-layouts: 42.8 us -> none  [source_term(): gathered = jnp.take(col_panel, slot_cols, axis=1)]
    dynamic_slice x49 -> x0, local copies, waits for them, and re-layouts: 39.9 us -> none  [the longest x32 29.1 us: add_source(): lax.dynamic_slice_in_dim(shard_piece, offset * rows_here, rows_here, 1)]
  transfers between devices with their start and end apart: 4 -> 0, of which waited for: 4 -> 0; matrix products, arithmetic and copies ran while one was open for 0% -> 0% of each run, Pallas kernels for 0% -> 0%
where the time goes in v1:
time: 179 us
  Pallas kernels  175 us (98%)
  local copies, waits for them, and re-layouts  2.94 us (2%)
    pallas_call x1, Pallas kernels, aggregate(): pl.pallas_call(aggregate_kernel, out_shape=jax.ShapeDtypeStruct((2048, 25...  76.6 us
    pallas_call x1, Pallas kernels, gather(): pl.pallas_call(gather_kernel, out_shape=jax.ShapeDtypeStruct((2, 4, 2, 16...  58.7 us
    pallas_call x1, Pallas kernels, tail(): pl.pallas_call(tail_kernel, out_shape=(jax.ShapeDtypeStruct((256, 256), j...  40 us

profile of v1, /device:TPU:1, one launch (start us, length us, event | category | flops | bytes accessed | tf_op | source)
XLA Modules:
  0.0 178.9 jit_solution(14603067317430946351)
XLA Ops:
  0.6 58.7 %gather.1 = bf16[2,4,2,16,4,2,32,128]{7,6,5,4,3,2,1,0:T(8,128)(2,1)} custom-call(bf16[32,2048]{1,0:T(8,128)(2,1)} %x_ref.1), custom_call_target="tpu_custom_call" | custom-call | tf_op jit(solution)/shard_map/gather/pallas_call | solution.py:158
  59.3 76.6 %aggregate.1 = bf16[2048,256]{1,0:T(8,128)(2,1)} custom-call(s32[16,48]{1,0:T(8,128)} %bitcast.9, s32[16,48]{1,0:T(8,128)} %bitcast.10, s32[16]{0:T(128)} %bitcast.11, bf16[16,16,256,128]{3,2,1,0:T(8,128)(2,1)} %bitcast.6, bf16[16,48,128,128]{3,2,1,0:T(8,128)(2,1)} %bitcast.7), custom_call_target="tpu_custom_call" | custom-call | tf_op jit(solution)/shard_map/aggregate/pallas_call | solution.py:223
  135.9 40.0 %tail.1 = (bf16[256,256]{1,0:T(8,128)(2,1)}, f32[32,256]{1,0:T(8,128)}) custom-call(bf16[8,256,256]{2,1,0:T(8,128)(2,1)} %bitcast.8, bf16[256,256]{1,0:T(8,128)(2,1)} %weight.1, bf16[256,256]{1,0:T(8,128)(2,1)} %cotangent.1), custom_call_target="tpu_custom_call" | custom-call | tf_op jit(solution)/shard_map/tail/pallas_call | solution.py:327
  176.0 1.6 copy.11
  177.5 1.4 copy.12

commit v2 on v1

--- a/solution.py
+++ b/solution.py
@@ -11,7 +11,11 @@
 MESH = pl.DeviceIdType.MESH
 TILE = 128
 ORDERS = (("x", "y", "z"), ("y", "z", "x"), ("z", "x", "y"))
-COLUMNS = ((0, 3, 6), (6, 8, 11), (11, 14, 16))
+CHUNKS = (
+    ((0, 2), (6, 8), (11, 13)),
+    ((2, 4), (8, 10), (13, 15)),
+    ((4, 6), (10, 11), (15, 16)),
+)
 MIB = 2**20
 
 
@@ -58,7 +62,7 @@
         return copy
 
 
-N_COPIES = 3 * 24
+N_COPIES = 9 * 21
 
 
 def gather_kernel(x_ref, full, own_sem, send_sem, recv_sem):
@@ -66,7 +70,7 @@
     sibling = moved(me, "c", 1)
     neighbours = [moved(me, d, by) for d in "xyz" for by in (1, 3)] + [sibling]
 
-    def region(at, lo, hi):
+    def region(at, span, rows=slice(None)):
         def index(value):
             if value is None:
                 return slice(None)
@@ -82,7 +86,7 @@
         else:
             x_lo, x_hi = pl.ds(x % 2, 1), pl.ds(x // 2, 1)
         return full.at[
-            x_lo, index(at["y"]), pl.ds(me["c"], 1), lo:hi, index(at["z"]), x_hi
+            x_lo, index(at["y"]), pl.ds(me["c"], 1), slice(*span), index(at["z"]), x_hi, rows
         ]
 
     barrier = pltpu.get_barrier_semaphore()
@@ -104,50 +108,61 @@
 
     net = Sender(send_sem, recv_sem)
     passed = []
-    state = [{} for _ in ORDERS]
-    for (d1, d2, d3), (lo, mid, hi), st in zip(ORDERS, COLUMNS, state):
-        st["a"] = net.start(region(me, lo, hi), moved(me, d1, 1))
-        st["b"] = net.start(region(me, lo, hi), moved(me, d1, 3))
-    for (d1, d2, d3), (lo, mid, hi), st in zip(ORDERS, COLUMNS, state):
-        st["a"].wait_recv()
-        st["ah"] = net.start(region(moved(me, d1, 3), lo, mid), moved(me, d1, 1))
-        st["b"].wait_recv()
-        st["bh"] = net.start(region(moved(me, d1, 1), mid, hi), moved(me, d1, 3))
-    for stage in (2, 3):
-        for (d1, d2, d3), (lo, mid, hi), st in zip(ORDERS, COLUMNS, state):
-            inner, ring = (d1, d2) if stage == 2 else (d2, d3)
-            held = {**me, d1: None}
-            if stage == 3:
-                held[d2] = None
-            if stage == 2:
-                st["ah"].wait_recv()
-                st["bh"].wait_recv()
-            else:
-                for name in ("p1", "m0", "pf", "mf"):
-                    st[name].wait_recv()
-                passed.append(net.start(region(held, lo, hi), sibling))
-            for name, by, half in (("p0", 1, 0), ("m1", 3, 1), ("p1", 1, 1), ("m0", 3, 0)):
-                st[name] = net.start(
-                    region({**held, inner: ("h", half)}, lo, hi), moved(me, ring, by)
-                )
-            st["held"], st["inner"], st["ring"] = held, inner, ring
-
-        def came(st, by, half):
-            return {**moved(st["held"], st["ring"], by), st["inner"]: ("h", half)}
-
-        for (lo, mid, hi), st in zip(COLUMNS, state):
-            st["p0"].wait_recv()
-            st["pf"] = net.start(region(came(st, 3, 0), lo, hi), moved(me, st["ring"], 1))
-            if stage == 3:
-                passed.append(net.start(region(came(st, 3, 0), lo, hi), sibling))
-            st["m1"].wait_recv()
-            st["mf"] = net.start(region(came(st, 1, 1), lo, hi), moved(me, st["ring"], 3))
-            if stage == 3:
-                passed.append(net.start(region(came(st, 1, 1), lo, hi), sibling))
-    for name, by, half in (("p1", 3, 1), ("m0", 1, 0), ("pf", 2, 0), ("mf", 2, 1)):
-        for (lo, mid, hi), st in zip(COLUMNS, state):
-            st[name].wait_recv()
-            passed.append(net.start(region(came(st, by, half), lo, hi), sibling))
+    lower, upper = slice(0, 16), slice(16, 32)
+    jobs = [[(order, span, {}) for order, span in zip(ORDERS, spans)] for spans in CHUNKS]
+
+    def to_sibling(at, span):
+        passed.append(net.start(region(at, span), sibling))
+
+    def open_ring(held, inner, ring, span, st):
+        for name, by, half in (("p0", 1, 0), ("m1", 3, 1), ("p1", 1, 1), ("m0", 3, 0)):
+            st[name] = net.start(region({**held, inner: ("h", half)}, span), moved(me, ring, by))
+
+    def pass_on(held, inner, ring, span, st):
+        st["p0"].wait_recv()
+        at = {**moved(held, ring, 3), inner: ("h", 0)}
+        st["pf"] = net.start(region(at, span), moved(me, ring, 1))
+        st["m1"].wait_recv()
+        at = {**moved(held, ring, 1), inner: ("h", 1)}
+        st["mf"] = net.start(region(at, span), moved(me, ring, 3))
+
+    for chunk in jobs:
+        for (d1, d2, d3), span, st in chunk:
+            st["a"] = net.start(region(me, span), moved(me, d1, 1))
+            st["b"] = net.start(region(me, span), moved(me, d1, 3))
+    for chunk in jobs:
+        for (d1, d2, d3), span, st in chunk:
+            st["a"].wait_recv()
+            st["ah"] = net.start(region(moved(me, d1, 3), span, lower), moved(me, d1, 1))
+            st["b"].wait_recv()
+            st["bh"] = net.start(region(moved(me, d1, 1), span, upper), moved(me, d1, 3))
+    for chunk in jobs:
+        for (d1, d2, d3), span, st in chunk:
+            st["ah"].wait_recv()
+            st["bh"].wait_recv()
+            open_ring({**me, d1: None}, d1, d2, span, st)
+    for chunk in jobs:
+        for (d1, d2, d3), span, st in chunk:
+            pass_on({**me, d1: None}, d1, d2, span, st)
+        for (d1, d2, d3), span, st in chunk:
+            for name in ("p1", "m0", "pf", "mf"):
+                st[name].wait_recv()
+            plane = {**me, d1: None, d2: None}
+            open_ring(plane, d2, d3, span, st)
+            to_sibling(plane, span)
+    for chunk in jobs:
+        for (d1, d2, d3), span, st in chunk:
+            pass_on({**me, d1: None, d2: None}, d2, d3, span, st)
+    for chunk in jobs:
+        for name, by in (("p1", 3), ("m0", 1)):
+            for (d1, d2, d3), span, st in chunk:
+                st[name].wait_recv()
+                to_sibling(moved({**me, d1: None, d2: None}, d3, by), span)
+        for name, half in (("pf", 0), ("mf", 1)):
+            for (d1, d2, d3), span, st in chunk:
+                st[name].wait_recv()
+                at = moved({**me, d1: None, d2: None}, d3, 2)
+                to_sibling({**at, d2: ("h", half)}, span)
     for copy in passed:
         copy.wait_recv()
     for copy in net.all:
@@ -170,67 +185,92 @@
     )(features)
 
 
-CHUNK = 16
+SLOTS = 16
+GROUP = 4
+BATCH = 32
 
 
 def aggregate_kernel(
-    rows_ref, cols_ref, counts_ref, full_hbm, tiles_hbm, out_ref, full, tiles, total, fsem, tsem
+    rows_ref, cols_ref, counts_ref, full_hbm, tiles_hbm, out_ref,
+    full, tiles, total, listed, fsem, tsem,
 ):
-    sources, slots = tiles_hbm.shape[:2]
+    sources = counts_ref.shape[0]
+    slots = tiles_hbm.shape[0] // sources
 
     def full_copy(s):
         return pltpu.make_async_copy(full_hbm.at[s], full.at[s], fsem.at[s])
 
-    def chunk_copy(s, c):
-        part = pl.ds(c * CHUNK, CHUNK)
-        return pltpu.make_async_copy(
-            tiles_hbm.at[s, part], tiles.at[s, part], tsem.at[s, c]
-        )
-
-    def over_chunks(s, act):
-        for c in range(slots // CHUNK):
-            pl.when(counts_ref[s] > c * CHUNK)(lambda c=c: act(chunk_copy(s, c)))
+    def tile_copies(s, act):
+        for c in range(slots // SLOTS):
+            part = pl.ds(s * slots + c * SLOTS, SLOTS)
+            copy = pltpu.make_async_copy(tiles_hbm.at[part], tiles.at[part], tsem.at[s, c])
+            pl.when(counts_ref[s] > c * SLOTS)(lambda copy=copy: act(copy))
 
     @pl.loop(0, sources)
     def _(s):
         full_copy(s).start()
-        over_chunks(s, lambda copy: copy.start())
+        tile_copies(s, lambda copy: copy.start())
 
     total[...] = jnp.zeros_like(total)
-
-    @pl.loop(0, sources)
-    def _(s):
-        full_copy(s).wait()
-        over_chunks(s, lambda copy: copy.wait())
-
-        @pl.loop(0, counts_ref[s])
-        def _(k):
-            at = pl.ds(pl.multiple_of(rows_ref[s, k] * TILE, TILE), TILE)
-            total[at, :] += lax.dot_general(
-                tiles[s, k],
-                full[s, cols_ref[s, k]],
-                (((1,), (1,)), ((), ())),
-                preferred_element_type=jnp.float32,
-            )
+    none = sources * slots
+    tiles[none] = jnp.zeros(tiles.shape[1:], tiles.dtype)
+
+    @pl.loop(0, sources // GROUP)
+    def _(g):
+        end = 0
+        for i in range(GROUP):
+            s = g * GROUP + i
+
+            def enter(j, carry, s=s, end=end):
+                for u in range(8):
+                    k = j * 8 + u
+                    code = (s * slots + k) * 4096 + (s * 16 + cols_ref[s, k]) * 16 + rows_ref[s, k]
+                    listed[end + k] = code
+                return carry
+
+            lax.fori_loop(0, (counts_ref[s] + 7) // 8, enter, 0)
+            end = end + counts_ref[s]
+        for u in range(BATCH):
+            listed[end + u] = none * 4096 + g * (GROUP * 16 * 16)
+        for i in range(GROUP):
+            s = g * GROUP + i
+            full_copy(s).wait()
+            tile_copies(s, lambda copy: copy.wait())
+
+        @pl.loop(0, (end + BATCH - 1) // BATCH)
+        def _(b):
+            codes = [listed[b * BATCH + u] for u in range(BATCH)]
+            products = [
+                lax.dot_general(
+                    full[(code >> 8) & 15, (code >> 4) & 15],
+                    tiles[code >> 12],
+                    (((1,), (1,)), ((), ())),
+                    preferred_element_type=jnp.float32,
+                )
+                for code in codes
+            ]
+            for code, product in zip(codes, products):
+                total[code & 15] += product
 
     out_ref[...] = total[...].astype(out_ref.dtype)
 
 
 def aggregate(rows, cols, counts, full, tiles):
-    sources, slots = tiles.shape[:2]
+    sources, slots = rows.shape
     smem = pl.BlockSpec(memory_space=pltpu.SMEM)
     hbm = pl.BlockSpec(memory_space=pl.ANY)
     return pl.pallas_call(
         aggregate_kernel,
-        out_shape=jax.ShapeDtypeStruct((2048, 256), jnp.bfloat16),
+        out_shape=jax.ShapeDtypeStruct((16, 256, TILE), jnp.bfloat16),
         in_specs=[smem, smem, smem, hbm, hbm],
         out_specs=pl.BlockSpec(memory_space=pltpu.VMEM),
         scratch_shapes=[
-            pltpu.VMEM(full.shape, jnp.bfloat16),
-            pltpu.VMEM(tiles.shape, jnp.bfloat16),
-            pltpu.VMEM((2048, 256), jnp.float32),
+            pltpu.VMEM((sources, 16, 256, TILE), jnp.bfloat16),
+            pltpu.VMEM((sources * slots + 1, TILE, TILE), jnp.bfloat16),
+            pltpu.VMEM((16, 256, TILE), jnp.float32),
+            pltpu.SMEM((GROUP * slots + BATCH + 8,), jnp.int32),
             pltpu.SemaphoreType.DMA((sources,)),
-            pltpu.SemaphoreType.DMA((sources, slots // CHUNK)),
+            pltpu.SemaphoreType.DMA((sources, slots // SLOTS)),
         ],
         compiler_params=pltpu.CompilerParams(vmem_limit_bytes=58 * MIB),
         name="aggregate",
@@ -274,13 +314,17 @@
         sent[i].wait_recv()
         summed = summed + held[i].astype(jnp.float32)
     nodes = summed.astype(jnp.bfloat16)
-    preact = lax.dot_general(
-        weight[...], nodes, (((1,), (1,)), ((), ())), preferred_element_type=jnp.float32
-    )
+    nodes = jnp.concatenate([nodes[0], nodes[1]], axis=1)
+    preact = jnp.dot(weight[...], nodes, preferred_element_type=jnp.float32)
     sigmoid = jax.nn.sigmoid(preact)
     act_ref[...] = (preact * sigmoid).astype(jnp.bfloat16)
     slope = cotangent[...].astype(jnp.float32) * sigmoid * (1.0 + preact * (1.0 - sigmoid))
-    local = jnp.dot(slope.astype(jnp.bfloat16), nodes, preferred_element_type=jnp.float32)
+    local = lax.dot_general(
+        slope.astype(jnp.bfloat16),
+        nodes,
+        (((1,), (1,)), ((), ())),
+        preferred_element_type=jnp.float32,
+    )
     terms[...] = local.reshape(terms.shape)
     sent_terms = []
     for i in range(1, 8):
@@ -333,7 +377,7 @@
         in_specs=[vmem] * 3,
         out_specs=(vmem, vmem),
         scratch_shapes=[
-            pltpu.VMEM((7, 256, 256), jnp.bfloat16),
+            pltpu.VMEM((7, 2, 256, TILE), jnp.bfloat16),
             pltpu.VMEM((8, 32, 256), jnp.float32),
             pltpu.VMEM((7, 32, 256), jnp.float32),
             pltpu.VMEM((8, 8, 128), jnp.float32),
@@ -349,7 +393,7 @@
 
 def shards(features, adj_tiles, tile_rows, tile_cols, counts, weight, cotangent):
     sources, slots = adj_tiles.shape[2:4]
-    tiles = adj_tiles.reshape(sources, slots, TILE, TILE)
+    tiles = adj_tiles.reshape(sources * slots, TILE, TILE)
     full = gather(features).reshape(sources, 16, 256, TILE)
     part = aggregate(
         tile_rows.reshape(sources, slots),
@@ -358,7 +402,7 @@
         full,
         tiles,
     )
-    return tail(part.reshape(8, 256, 256), weight, cotangent)
+    return tail(part.reshape(8, 2, 256, TILE), weight, cotangent)
 
 
 def solution(mesh):

time: 179 us -> 121 us (0.68)
  Pallas kernels: 175 us -> 117 us
    pallas_call x1, Pallas kernels: 76.6 us -> 13.2 us  [aggregate(): pl.pallas_call(aggregate_kernel, out_shape=jax.ShapeDtypeStruct((16, 256,...]
    pallas_call x1, Pallas kernels: 58.7 us -> 63.5 us  [gather(): pl.pallas_call(gather_kernel, out_shape=jax.ShapeDtypeStruct((2, 4, 2, 16...]
where the time goes in v2:
time: 121 us
  Pallas kernels  117 us (97%)
  local copies, waits for them, and re-layouts  2.94 us (2%)
    pallas_call x1, Pallas kernels, gather(): pl.pallas_call(gather_kernel, out_shape=jax.ShapeDtypeStruct((2, 4, 2, 16...  63.5 us
    pallas_call x1, Pallas kernels, tail(): pl.pallas_call(tail_kernel, out_shape=(jax.ShapeDtypeStruct((256, 256), j...  40.8 us
    pallas_call x1, Pallas kernels, aggregate(): pl.pallas_call(aggregate_kernel, out_shape=jax.ShapeDtypeStruct((16, 256,...  13.2 us
    unnamed x2, local copies, waits for them, and re-layouts  2.94 us

profile of v2, /device:TPU:1, one launch (start us, length us, event | category | flops | bytes accessed | tf_op | source)
XLA Modules:
  0.0 121.0 jit_solution(5391919420083175959)
XLA Ops:
  0.6 63.5 %gather.1 = bf16[2,4,2,16,4,2,32,128]{7,6,5,4,3,2,1,0:T(8,128)(2,1)} custom-call(bf16[32,2048]{1,0:T(8,128)(2,1)} %x_ref.1), custom_call_target="tpu_custom_call" | custom-call | tf_op jit(solution)/shard_map/gather/pallas_call | solution.py:173
  64.1 13.2 %aggregate.1 = bf16[16,256,128]{2,1,0:T(8,128)(2,1)} custom-call(s32[16,48]{1,0:T(8,128)} %bitcast.9, s32[16,48]{1,0:T(8,128)} %bitcast.10, s32[16]{0:T(128)} %bitcast.11, bf16[16,16,256,128]{3,2,1,0:T(8,128)(2,1)} %bitcast.6, bf16[768,128,128]{2,1,0:T(8,128)(2,1)} %bitcast.7), custom_call_target="tpu_custom_call" | custom-call | tf_op jit(solution)/shard_map/aggregate/pallas_call | solution.py:262
  77.3 40.8 %tail.1 = (bf16[256,256]{1,0:T(8,128)(2,1)}, f32[32,256]{1,0:T(8,128)}) custom-call(bf16[8,2,256,128]{3,2,1,0:T(8,128)(2,1)} %bitcast.8, bf16[256,256]{1,0:T(8,128)(2,1)} %weight.1, bf16[256,256]{1,0:T(8,128)(2,1)} %cotangent.1), custom_call_target="tpu_custom_call" | custom-call | tf_op jit(solution)/shard_map/tail/pallas_call | solution.py:371
  118.1 1.6 %copy.11 = bf16[256,256]{1,0:T(8,128)(2,1)} copy(bf16[256,256]{1,0:T(8,128)(2,1)} %get-tuple-element.4) | data formatting | bytes 262144
  119.7 1.4 %copy.12 = f32[32,256]{1,0:T(8,128)} copy(f32[32,256]{1,0:T(8,128)} %get-tuple-element.5) | data formatting | bytes 65536

commit v3 on v1

v3 whole, which is shorter than its diff:
```python
import functools
import math

import jax
import jax.numpy as jnp
from jax import lax
from jax.experimental import pallas as pl
from jax.experimental.pallas import tpu as pltpu
from jax.sharding import PartitionSpec as P

MESH = pl.DeviceIdType.MESH
TILE = 128
ORDERS = (("x", "y", "z"), ("y", "z", "x"), ("z", "x", "y"))
COLUMNS = ((0, 6), (6, 11), (11, 16))
MIB = 2**20


EARLY = 24


def in_vmem(array):
    return pltpu.with_memory_space_constraint(array, pltpu.VMEM)


def in_hbm(array):
    return pltpu.with_memory_space_constraint(array, pltpu.HBM)


def place():
    blk = lax.axis_index("blk")
    feat = lax.axis_index("feat")
    return {
        "x": (feat % 2) * 2 + blk // 8,
        "y": (blk // 2) % 4,
        "z": feat // 2,
        "c": blk % 2,
    }


def device(at):
    return {
        "blk": ((at["x"] % 2) * 4 + at["y"]) * 2 + at["c"],
        "feat": at["z"] * 2 + at["x"] // 2,
    }


def moved(at, dim, by):
    return {**at, dim: (at[dim] + by) % (2 if dim == "c" else 4)}


class Sender:
    def __init__(self, send_sem, recv_sem):
        self.send_sem, self.recv_sem, self.used, self.all = send_sem, recv_sem, 0, []

    def start(self, ref, to):
        i = self.used
        self.used += 1
        copy = pltpu.make_async_remote_copy(
            src_ref=ref,
            dst_ref=ref,
            send_sem=self.send_sem.at[i],
            recv_sem=self.recv_sem.at[i],
            device_id=device(to),
            device_id_type=MESH,
        )
        self.all.append(copy)
        copy.start()
        return copy


N_COPIES = 3 * 50


class Ring:
    def __init__(self, net, me, order, span, full):
        self.net, self.me, self.order, self.span, self.full = net, me, order, span, full
        self.first, self.size = span[0] * 128, span[1] - span[0]
        self.p1, self.p2, self.p3 = (me[d] for d in order)
        self.went, self.passed = {}, []

    def place(self, by1, by2, by3):
        at = (self.me["c"] * 4 + (self.p3 + by3) % 4) * 4 + (self.p2 + by2) % 4
        return self.first + (at * 4 + by1) * self.size

    def block(self, by1, by2=0, by3=0):
        return self.full.at[pl.ds(self.place((self.p1 + by1) % 4, by2, by3), self.size)]

    def line(self, by3, by2):
        return self.full.at[pl.ds(self.place(0, by2, by3), 4 * self.size)]

    def spread(self, by1):
        for name, by in (("p", 1), ("m", 3)):
            self.send(f"{name}{by1}", self.block(by1), 2, by)
        for name, by in (("u0", 1), ("v0", 3)):
            self.send(f"{name}{by1}", self.block(by1), 3, by)

    def out(self, by2):
        self.send(f"u{by2}", self.line(0, by2), 3, 1)
        self.send(f"v{by2}", self.line(0, by2), 3, 3)
        self.share(self.line(0, by2))

    def send(self, name, ref, step, by):
        to = moved(self.me, self.order[step - 1], by)
        self.went[name] = self.net.start(ref, to)

    def came(self, *names):
        for name in names:
            self.went[name].wait_recv()

    def share(self, ref):
        self.passed.append(self.net.start(ref, moved(self.me, "c", 1)))


def gather_kernel(
    x_ref, tiles_hbm, rows_hbm, cols_hbm, full, tiles, codes,
    rows, cols, own_sem, slot_sem, tile_sem, send_sem, recv_sem,
):
    me = place()
    sibling = moved(me, "c", 1)
    neighbours = [moved(me, d, by) for d in "xyz" for by in (1, 3)] + [sibling]
    barrier = pltpu.get_barrier_semaphore()
    for other in neighbours:
        pl.semaphore_signal(barrier, inc=1, device_id=device(other), device_id_type=MESH)
    slot_loads = [
        pltpu.make_async_copy(rows_hbm, rows, slot_sem.at[0]),
        pltpu.make_async_copy(cols_hbm, cols, slot_sem.at[1]),
    ]
    for copy in slot_loads:
        copy.start()
    net = Sender(send_sem, recv_sem)
    rings = [
        Ring(net, me, order, span, full)
        for order, span in zip(ORDERS, COLUMNS)
    ]
    own = []
    for r in rings:
        for i, ct in enumerate(range(*r.span)):
            own.append(
                pltpu.make_async_copy(
                    x_ref.at[:, ct * TILE : (ct + 1) * TILE],
                    r.full.at[r.place(r.p1, 0, 0) + i],
                    own_sem.at[ct],
                )
            )
            own[-1].start()
    for copy in own:
        copy.wait()
    pl.semaphore_wait(barrier, len(neighbours))

    lower, upper = (slice(None), slice(0, 16)), (slice(None), slice(16, 32))
    for r in rings:
        r.send("a", r.block(0), 1, 1)
        r.send("b", r.block(0), 1, 3)
    for r in rings:
        r.spread(0)
    sources = rows.shape[0]
    slots = tiles_hbm.shape[0] // sources
    loads = []
    for i in range(sources):
        copy = pltpu.make_async_copy(
            tiles_hbm.at[i * slots : i * slots + EARLY],
            tiles.at[i * EARLY : (i + 1) * EARLY],
            tile_sem.at[i],
        )
        loads.append(copy)
        loads[-1].start()
    for copy in slot_loads:
        copy.wait()
    codes[...] = slot_codes(rows[...], cols[...])
    for r in rings:
        r.came("a")
        r.send("af", r.block(3).at[lower], 1, 1)
        r.came("b")
        r.send("bf", r.block(1).at[upper], 1, 3)
    for r in rings:
        r.spread(3)
        r.spread(1)
    for r in rings:
        r.came("p0")
        r.send("pf0", r.block(0, 3), 2, 1)
    for r in rings:
        r.came("af", "bf")
        r.spread(2)
        r.share(r.line(0, 0))
    for r in rings:
        r.came("p3")
        r.send("pf3", r.block(3, 3), 2, 1)
        r.came("m1")
        r.send("mf1", r.block(1, 1), 2, 3)
    for r in rings:
        r.came("m0", "m3", "m2")
        r.send("mf2", r.block(2, 1), 2, 3)
        r.out(1)
        r.came("p1", "p2")
        r.out(3)
    for r in rings:
        r.came("u00", "u03", "u01", "u02")
        r.send("u0f", r.line(3, 0), 3, 1)
        r.share(r.line(3, 0))
        r.came("v00", "v03", "v01", "v02")
        r.share(r.line(1, 0))
    for r in rings:
        r.came("pf0", "pf3", "mf1", "mf2")
        r.out(2)
    for name, by3, by2, on in (
        ("v1", 1, 1, 3), ("u3", 3, 3, 1), ("u1", 3, 1, 0), ("v3", 1, 3, 0),
        ("v2", 1, 2, 3), ("u2", 3, 2, 0),
    ):
        for r in rings:
            r.came(name)
            if on:
                r.send(name + "f", r.line(by3, by2), 3, on)
            r.share(r.line(by3, by2))
    for name, by2 in (("u0f", 0), ("u3f", 3), ("v1f", 1), ("v2f", 2)):
        for r in rings:
            r.came(name)
            r.share(r.line(2, by2))
    for r in rings:
        for copy in r.passed:
            copy.wait_recv()
    for copy in net.all:
        copy.wait_send()
    for copy in loads:
        copy.wait()


def slot_codes(rows, cols):
    source = lax.broadcasted_iota(jnp.int32, rows.shape, 0)
    slot = lax.broadcasted_iota(jnp.int32, rows.shape, 1)
    c, y, x = source & 1, (source >> 1) & 3, source >> 3
    at = {"c": c, "x": x, "y": y, "z": jnp.zeros_like(x)}
    block, order = 0, 0
    for i, (dims, (lo, hi)) in enumerate(zip(ORDERS, COLUMNS)):
        d1, d2, d3 = (at[d] for d in dims)
        here = lo * 128 + (((c * 4 + d3) * 4 + d2) * 4 + d1) * (hi - lo) + cols - lo
        block, order = jnp.where(cols >= lo, here, block), jnp.where(cols >= lo, i, order)
    tile = source * EARLY + jnp.where(slot < EARLY, slot, slot - EARLY)
    return (tile << 18) | (block << 7) | (order << 5) | rows


def strides(dim):
    return [(hi - lo) * 4 ** dims.index(dim) for dims, (lo, hi) in zip(ORDERS, COLUMNS)]


def gather(features, tiles, rows, cols):
    hbm = pl.BlockSpec(memory_space=pltpu.HBM)
    vmem = pl.BlockSpec(memory_space=pltpu.VMEM)
    dma = pltpu.SemaphoreType.DMA
    return pl.pallas_call(
        gather_kernel,
        out_shape=(
            pltpu.VMEM((2048, 32, TILE), jnp.bfloat16),
            pltpu.VMEM((tiles.shape[0] // 2, TILE, TILE), jnp.bfloat16),
            jax.ShapeDtypeStruct(rows.shape, jnp.int32),
        ),
        in_specs=[hbm] * 4,
        out_specs=(vmem, vmem, vmem),
        scratch_shapes=[
            pltpu.VMEM(rows.shape, jnp.int32), pltpu.VMEM(cols.shape, jnp.int32),
            dma((16,)), dma((2,)), dma((rows.shape[0],)), dma((N_COPIES,)), dma((N_COPIES,)),
        ],
        compiler_params=pltpu.CompilerParams(
            collective_id=0, has_side_effects=True, vmem_limit_bytes=2 * MIB
        ),
        name="gather",
    )(*(in_hbm(a) for a in (features, tiles, rows, cols)))


BATCH = 32


def aggregate_kernel(
    codes, counts, full, early, tiles_hbm, out_ref, late, total, listed, late_sem
):
    sources, slots = codes.shape

    def late_copy(s):
        return pltpu.make_async_copy(
            tiles_hbm.at[pl.ds(s * slots + EARLY, EARLY)],
            late.at[pl.ds(s * EARLY, EARLY)],
            late_sem.at[s],
        )

    @pl.loop(0, sources)
    def _(s):
        pl.when(counts[s] > EARLY)(lambda: late_copy(s).start())

    total[...] = jnp.zeros_like(total)

    def enlist(first):
        def enter(s, end):
            live = jnp.clip(counts[s] - first, 0, EARLY)

            def eight(j, carry):
                for u in range(8):
                    listed[end + j * 8 + u] = codes[s, first + j * 8 + u]
                return carry

            lax.fori_loop(0, (live + 7) >> 3, eight, 0)
            return end + live

        end = lax.fori_loop(0, sources, enter, 0)
        for u in range(BATCH):
            listed[end + u] = out_ref.shape[0]
        return (end + BATCH - 1) // BATCH

    def pick(order, values):
        return jnp.where(order == 0, values[0], jnp.where(order == 1, values[1], values[2]))

    def panel(code):
        block, order = (code >> 7) & 2047, (code >> 5) & 3
        step_z, step_x = pick(order, strides("z")), pick(order, strides("x")) * 2
        parts = [full[block + z * step_z + x_hi * step_x] for z in range(4) for x_hi in range(2)]
        return jnp.concatenate(parts, axis=0)

    def work(steps, tiles):
        @pl.loop(0, steps)
        def _(b):
            for part in range(0, BATCH, BATCH // 2):
                entries = [listed[b * BATCH + part + u] for u in range(BATCH // 2)]
                products = [
                    lax.dot_general(
                        panel(code),
                        tiles[code >> 18],
                        (((1,), (1,)), ((), ())),
                        preferred_element_type=jnp.float32,
                    )
                    for code in entries
                ]
                for code, product in zip(entries, products):
                    total[code & 31] += product

    work(enlist(0), early)

    @pl.loop(0, sources)
    def _(s):
        pl.when(counts[s] > EARLY)(lambda: late_copy(s).wait())

    work(enlist(EARLY), late)
    out_ref[...] = total[: out_ref.shape[0]].astype(out_ref.dtype)


def aggregate(codes, counts, full, early, tiles):
    smem = pl.BlockSpec(memory_space=pltpu.SMEM)
    vmem = pl.BlockSpec(memory_space=pltpu.VMEM)
    return pl.pallas_call(
        aggregate_kernel,
        out_shape=pltpu.VMEM((16, 256, TILE), jnp.bfloat16),
        in_specs=[smem, smem, vmem, vmem, pl.BlockSpec(memory_space=pltpu.HBM)],
        out_specs=vmem,
        scratch_shapes=[
            pltpu.VMEM(early.shape, jnp.bfloat16),
            pltpu.VMEM((17, 256, TILE), jnp.float32),
            pltpu.SMEM((codes.size // 2 + BATCH + 8,), jnp.int32),
            pltpu.SemaphoreType.DMA((codes.shape[0],)),
        ],
        compiler_params=pltpu.CompilerParams(vmem_limit_bytes=17 * MIB),
        name="aggregate",
    )(codes, counts, in_vmem(full), in_vmem(early), in_hbm(tiles))


def tail_kernel(
    part, weight, cotangent, act_ref, sums_ref,
    held, terms, terms_in, psem, pin, tsem, tin, msem, min_,
):
    blk, feat = lax.axis_index("blk"), lax.axis_index("feat")
    barrier = pltpu.get_barrier_semaphore()
    for i in range(1, 8):
        pl.semaphore_signal(
            barrier, inc=1, device_id={"feat": (feat + i) % 8}, device_id_type=MESH
        )
    for i in range(1, 16):
        pl.semaphore_signal(
            barrier, inc=1, device_id={"blk": (blk + i) % 16}, device_id_type=MESH
        )
    pl.semaphore_wait(barrier, 22)

    def remote(src, dst, send, recv, to):
        copy = pltpu.make_async_remote_copy(
            src_ref=src, dst_ref=dst, send_sem=send, recv_sem=recv,
            device_id=to, device_id_type=MESH,
        )
        copy.start()
        return copy

    sent = []
    for i in range(1, 8):
        to = (feat + i) % 8
        sent.append(
            remote(part.at[to], held.at[i - 1], psem.at[i - 1], pin.at[i - 1], {"feat": to})
        )
    summed = part[feat].astype(jnp.float32)
    for i in range(7):
        sent[i].wait_recv()
        summed = summed + held[i].astype(jnp.float32)
    nodes = summed.astype(jnp.bfloat16)
    nodes = jnp.concatenate([nodes[0], nodes[1]], axis=1)
    preact = jnp.dot(weight[...], nodes, preferred_element_type=jnp.float32)
    sigmoid = jax.nn.sigmoid(preact)
    act_ref[...] = (preact * sigmoid).astype(jnp.bfloat16)
    slope = cotangent[...].astype(jnp.float32) * sigmoid * (1.0 + preact * (1.0 - sigmoid))
    local = lax.dot_general(
        slope.astype(jnp.bfloat16),
        nodes,
        (((1,), (1,)), ((), ())),
        preferred_element_type=jnp.float32,
    )
    terms[...] = local.reshape(terms.shape)
    sent_terms = []
    for i in range(1, 8):
        to = (feat + i) % 8
        sent_terms.append(
            remote(terms.at[to], terms_in.at[i - 1], tsem.at[i - 1], tin.at[i - 1], {"feat": to})
        )
    share = terms[feat]
    for i in range(7):
        sent_terms[i].wait_recv()
        share = share + terms_in[i]
    sums_ref[blk] = share.astype(sums_ref.dtype)
    sent_sums = []
    for i in range(1, 16):
        sent_sums.append(
            remote(
                sums_ref.at[blk], sums_ref.at[blk], msem.at[i - 1], min_.at[i - 1],
                {"blk": (blk + i) % 16},
            )
        )
    for copy in sent_sums:
        copy.wait_recv()
    for copy in sent + sent_terms + sent_sums:
        copy.wait_send()


def tail(part, weight, cotangent):
    vmem = pl.BlockSpec(memory_space=pltpu.VMEM)
    dma = pltpu.SemaphoreType.DMA
    return pl.pallas_call(
        tail_kernel,
        out_shape=(
            pltpu.VMEM((256, 256), jnp.bfloat16),
            pltpu.VMEM((16, 32, 256), jnp.bfloat16),
        ),
        in_specs=[vmem] * 3,
        out_specs=(vmem, vmem),
        scratch_shapes=[
            pltpu.VMEM((7, 2, 256, TILE), jnp.bfloat16),
            pltpu.VMEM((8, 32, 256), jnp.float32),
            pltpu.VMEM((7, 32, 256), jnp.float32),
            dma((7,)), dma((7,)), dma((7,)), dma((7,)), dma((15,)), dma((15,)),
        ],
        compiler_params=pltpu.CompilerParams(collective_id=1, has_side_effects=True),
        name="tail",
    )(in_vmem(part), weight, cotangent)


def finish_kernel(act, sums, act_ref, grad_ref):
    act_ref[...] = act[...]
    grad_ref[...] = jnp.sum(sums[...].astype(jnp.float32), axis=0) * (1.0 / math.sqrt(32768))


def finish(act, sums):
    vmem = pl.BlockSpec(memory_space=pltpu.VMEM)
    return pl.pallas_call(
        finish_kernel,
        out_shape=(
            jax.ShapeDtypeStruct(act.shape, act.dtype),
            jax.ShapeDtypeStruct(sums.shape[1:], jnp.float32),
        ),
        in_specs=[vmem] * 2,
        out_specs=(vmem, vmem),
        name="finish",
    )(in_vmem(act), in_vmem(sums))


def shards(features, adj_tiles, tile_rows, tile_cols, counts, weight, cotangent):
    sources, slots = adj_tiles.shape[2:4]
    tiles = adj_tiles.reshape(sources * slots, TILE, TILE)
    rows, cols = (a.reshape(sources, slots) for a in (tile_rows, tile_cols))
    full, early, codes = gather(features, tiles, rows, cols)
    part = aggregate(codes, counts.reshape(sources), full, early, tiles)
    part = part.reshape(8, 2, 256, TILE)
    return finish(*tail(part, weight, cotangent))


def solution(mesh):
    in_specs = (
        P("feat", "blk"),
        P("blk", "feat", None, None, None, None),
        P("blk", "feat", None, None),
        P("blk", "feat", None, None),
        P("blk", "feat", None),
        P(),
        P(None, ("blk", "feat")),
    )
    out_specs = (P(None, ("blk", "feat")), P("feat", None))
    return jax.shard_map(shards, mesh=mesh, in_specs=in_specs, out_specs=out_specs, check_vma=False)
```

time: 179 us -> 93.6 us (0.52)
  Pallas kernels: 175 us -> 92.7 us
  local copies, waits for them, and re-layouts: 2.94 us -> 0.01 us
    pallas_call x3 -> x4, Pallas kernels: 175 us -> 92.7 us  [the longest x1 48.3 us: gather(): pl.pallas_call(gather_kernel, out_shape=(pltpu.VMEM((2048, 32, TILE), jnp...]
    unnamed x2, local copies, waits for them, and re-layouts: 2.94 us -> 0.01 us
where the time goes in v3:
time: 93.6 us; the launch traced here: 93.4 us
  Pallas kernels  92.7 us (99%)
    pallas_call x1, Pallas kernels, gather(): pl.pallas_call(gather_kernel, out_shape=(pltpu.VMEM((2048, 32, TILE), jnp...  48.3 us
    pallas_call x1, Pallas kernels, tail(): pl.pallas_call(tail_kernel, out_shape=(pltpu.VMEM((256, 256), jnp.bfloat1...  38.2 us
    pallas_call x1, Pallas kernels, aggregate(): pl.pallas_call(aggregate_kernel, out_shape=pltpu.VMEM((16, 256, TILE), jn...  5.5 us

profile of v3, /device:TPU:1, one launch (start us, length us, event | category | flops | bytes accessed | tf_op | source)
XLA Modules:
  0.0 93.4 jit_solution(4901734271217535778)
XLA Ops:
  0.6 0.0 copy-start
  0.6 48.3 %gather.1 = (bf16[2048,32,128]{2,1,0:T(8,128)(2,1)S(1)}, bf16[384,128,128]{2,1,0:T(8,128)(2,1)S(1)}, s32[16,48]{1,0:T(8,128)S(1)}) custom-call(bf16[32,2048]{1,0:T(8,128)(2,1)} %x_ref.1, bf16[768,128,128]{2,1,0:T(8,128)(2,1)} %bitcast.7, s32[16,48]{1,0:T(8,128)} %bitcast.9, s32[16,48]{1,0:T(8,128)} %bitcast.10), custom_call_target="tpu_custom_call" | custom-call | tf_op jit(solution)/shard_map/gather/pallas_call | solution.py:249
  49.0 0.0 copy-done
  49.0 5.5 %aggregate.1 = bf16[16,256,128]{2,1,0:T(8,128)(2,1)S(1)} custom-call(s32[16,48]{1,0:T(8,128)S(1)} %get-tuple-element.7.codes, s32[16]{0:T(128)S(1)} %bitcast.6, bf16[2048,32,128]{2,1,0:T(8,128)(2,1)S(1)} %get-tuple-element.8.full, bf16[384,128,128]{2,1,0:T(8,128)(2,1)S(1)} %get-tuple-element.9.early, bf16[768,128,128]{2,1,0:T(8,128)(2,1)} %bitcast.8), custom_call_target="tpu_custom_call" | custom-call | tf_op jit(solution)/shard_map/aggregate/pallas_call | solution.py:346
  54.5 38.2 %tail.1 = (bf16[256,256]{1,0:T(8,128)(2,1)S(1)}, bf16[16,32,256]{2,1,0:T(8,128)(2,1)S(1)}) custom-call(bf16[8,2,256,128]{3,2,1,0:T(8,128)(2,1)S(1)} %bitcast.5, bf16[256,256]{1,0:T(8,128)(2,1)} %weight.1, bf16[256,256]{1,0:T(8,128)(2,1)} %cotangent.1), custom_call_target="tpu_custom_call" | custom-call | tf_op jit(solution)/shard_map/tail/pallas_call | solution.py:437
  92.7 0.7 finish.1
Async XLA Ops:
  0.6 48.4 %copy-start = (s32[1,1,16]{2,1,0:T(1,128)S(1)}, s32[1,1,16]{2,1,0:T(1,128)}, u32[]{:S(2)}) copy-start(s32[1,1,16]{2,1,0:T(1,128)} %param.11) | copy-start | bytes 196

commit v4 on v3

--- a/solution.py
+++ b/solution.py
@@ -11,7 +11,7 @@
 MESH = pl.DeviceIdType.MESH
 TILE = 128
 ORDERS = (("x", "y", "z"), ("y", "z", "x"), ("z", "x", "y"))
-COLUMNS = ((0, 6), (6, 11), (11, 16))
+COLUMNS = (((0, 6), (6, 11), (11, 16)), ((0, 5), (5, 11), (11, 16)))
 MIB = 2**20
 
 
@@ -52,35 +52,44 @@
     def __init__(self, send_sem, recv_sem):
         self.send_sem, self.recv_sem, self.used, self.all = send_sem, recv_sem, 0, []
 
-    def start(self, ref, to):
+    def start(self, ref, to, comes=None):
         i = self.used
         self.used += 1
-        copy = pltpu.make_async_remote_copy(
-            src_ref=ref,
-            dst_ref=ref,
-            send_sem=self.send_sem.at[i],
-            recv_sem=self.recv_sem.at[i],
-            device_id=device(to),
-            device_id_type=MESH,
-        )
+
+        def copy_of(ref):
+            return pltpu.make_async_remote_copy(
+                src_ref=ref,
+                dst_ref=ref,
+                send_sem=self.send_sem.at[i],
+                recv_sem=self.recv_sem.at[i],
+                device_id=device(to),
+                device_id_type=MESH,
+            )
+
+        copy = copy_of(ref)
         self.all.append(copy)
         copy.start()
-        return copy
+        return copy if comes is None else copy_of(comes)
 
 
 N_COPIES = 3 * 50
 
 
+def first_block(core, span):
+    return core * 1024 + span[0] * 64
+
+
 class Ring:
-    def __init__(self, net, me, order, span, full):
-        self.net, self.me, self.order, self.span, self.full = net, me, order, span, full
-        self.first, self.size = span[0] * 128, span[1] - span[0]
-        self.p1, self.p2, self.p3 = (me[d] for d in order)
+    def __init__(self, net, me, core, which, full):
+        self.net, self.me, self.core, self.which, self.full = net, me, core, which, full
+        self.order, self.span = ORDERS[which], COLUMNS[core][which]
+        self.size = self.span[1] - self.span[0]
+        self.p1, self.p2, self.p3 = (me[d] for d in self.order)
         self.went, self.passed = {}, []
 
     def place(self, by1, by2, by3):
-        at = (self.me["c"] * 4 + (self.p3 + by3) % 4) * 4 + (self.p2 + by2) % 4
-        return self.first + (at * 4 + by1) * self.size
+        at = ((self.p3 + by3) % 4 * 4 + (self.p2 + by2) % 4) * 4 + by1
+        return first_block(self.core, self.span) + at * self.size
 
     def block(self, by1, by2=0, by3=0):
         return self.full.at[pl.ds(self.place((self.p1 + by1) % 4, by2, by3), self.size)]
@@ -94,10 +103,9 @@
         for name, by in (("u0", 1), ("v0", 3)):
             self.send(f"{name}{by1}", self.block(by1), 3, by)
 
-    def out(self, by2):
-        self.send(f"u{by2}", self.line(0, by2), 3, 1)
-        self.send(f"v{by2}", self.line(0, by2), 3, 3)
-        self.share(self.line(0, by2))
+    def out(self, by2, *bys):
+        for by in bys:
+            self.send(f"{'u' if by == 1 else 'v'}{by2}", self.line(0, by2), 3, by)
 
     def send(self, name, ref, step, by):
         to = moved(self.me, self.order[step - 1], by)
@@ -107,8 +115,10 @@
         for name in names:
             self.went[name].wait_recv()
 
-    def share(self, ref):
-        self.passed.append(self.net.start(ref, moved(self.me, "c", 1)))
+    def share(self, by3, by2):
+        to = moved(self.me, "c", 1)
+        theirs = Ring(self.net, self.me, 1 - self.core, self.which, self.full)
+        self.passed.append(self.net.start(self.line(by3, by2), to, theirs.line(by3, by2)))
 
 
 def gather_kernel(
@@ -127,11 +137,21 @@
     ]
     for copy in slot_loads:
         copy.start()
+    for core in range(2):
+        pl.when(me["c"] == core)(
+            functools.partial(
+                gather_core, core, me, neighbours, barrier, x_ref, tiles_hbm, full, tiles, codes,
+                rows, cols, slot_loads, own_sem, tile_sem, send_sem, recv_sem,
+            )
+        )
+
+
+def gather_core(
+    core, me, neighbours, barrier, x_ref, tiles_hbm, full, tiles, codes,
+    rows, cols, slot_loads, own_sem, tile_sem, send_sem, recv_sem,
+):
     net = Sender(send_sem, recv_sem)
-    rings = [
-        Ring(net, me, order, span, full)
-        for order, span in zip(ORDERS, COLUMNS)
-    ]
+    rings = [Ring(net, me, core, which, full) for which in range(3)]
     own = []
     for r in rings:
         for i, ct in enumerate(range(*r.span)):
@@ -181,7 +201,7 @@
     for r in rings:
         r.came("af", "bf")
         r.spread(2)
-        r.share(r.line(0, 0))
+        r.share(0, 0)
     for r in rings:
         r.came("p3")
         r.send("pf3", r.block(3, 3), 2, 1)
@@ -190,18 +210,22 @@
     for r in rings:
         r.came("m0", "m3", "m2")
         r.send("mf2", r.block(2, 1), 2, 3)
-        r.out(1)
+        r.out(1, 3)
         r.came("p1", "p2")
-        r.out(3)
+        r.out(3, 1, 3)
+        r.out(1, 1)
+        r.share(0, 1)
+        r.share(0, 3)
     for r in rings:
         r.came("u00", "u03", "u01", "u02")
         r.send("u0f", r.line(3, 0), 3, 1)
-        r.share(r.line(3, 0))
+        r.share(3, 0)
         r.came("v00", "v03", "v01", "v02")
-        r.share(r.line(1, 0))
+        r.share(1, 0)
     for r in rings:
         r.came("pf0", "pf3", "mf1", "mf2")
-        r.out(2)
+        r.out(2, 3, 1)
+        r.share(0, 2)
     for name, by3, by2, on in (
         ("v1", 1, 1, 3), ("u3", 3, 3, 1), ("u1", 3, 1, 0), ("v3", 1, 3, 0),
         ("v2", 1, 2, 3), ("u2", 3, 2, 0),
@@ -210,11 +234,11 @@
             r.came(name)
             if on:
                 r.send(name + "f", r.line(by3, by2), 3, on)
-            r.share(r.line(by3, by2))
+            r.share(by3, by2)
     for name, by2 in (("u0f", 0), ("u3f", 3), ("v1f", 1), ("v2f", 2)):
         for r in rings:
             r.came(name)
-            r.share(r.line(2, by2))
+            r.share(2, by2)
     for r in rings:
         for copy in r.passed:
             copy.wait_recv()
@@ -228,18 +252,26 @@
     source = lax.broadcasted_iota(jnp.int32, rows.shape, 0)
     slot = lax.broadcasted_iota(jnp.int32, rows.shape, 1)
     c, y, x = source & 1, (source >> 1) & 3, source >> 3
-    at = {"c": c, "x": x, "y": y, "z": jnp.zeros_like(x)}
-    block, order = 0, 0
-    for i, (dims, (lo, hi)) in enumerate(zip(ORDERS, COLUMNS)):
-        d1, d2, d3 = (at[d] for d in dims)
-        here = lo * 128 + (((c * 4 + d3) * 4 + d2) * 4 + d1) * (hi - lo) + cols - lo
-        block, order = jnp.where(cols >= lo, here, block), jnp.where(cols >= lo, i, order)
+    at = {"x": x, "y": y, "z": jnp.zeros_like(x)}
+    block, layout = 0, 0
+    for core in range(2):
+        for i, (dims, span) in enumerate(zip(ORDERS, COLUMNS[core])):
+            d1, d2, d3 = (at[d] for d in dims)
+            size = span[1] - span[0]
+            here = first_block(core, span) + ((d3 * 4 + d2) * 4 + d1) * size + cols - span[0]
+            inside = (c == core) & (cols >= span[0])
+            block = jnp.where(inside, here, block)
+            layout = jnp.where(inside, core * 3 + i, layout)
     tile = source * EARLY + jnp.where(slot < EARLY, slot, slot - EARLY)
-    return (tile << 18) | (block << 7) | (order << 5) | rows
+    return (tile << 19) | (block << 8) | (layout << 5) | rows
 
 
 def strides(dim):
-    return [(hi - lo) * 4 ** dims.index(dim) for dims, (lo, hi) in zip(ORDERS, COLUMNS)]
+    return [
+        (hi - lo) * 4 ** dims.index(dim)
+        for columns in COLUMNS
+        for dims, (lo, hi) in zip(ORDERS, columns)
+    ]
 
 
 def gather(features, tiles, rows, cols):
@@ -270,7 +302,8 @@
 
 
 def aggregate_kernel(
-    codes, counts, full, early, tiles_hbm, out_ref, late, total, listed, late_sem
+    codes, counts, full, early, tiles_hbm, out_ref,
+    late, total, listed, steps_z, steps_x, late_sem,
 ):
     sources, slots = codes.shape
 
@@ -304,12 +337,13 @@
             listed[end + u] = out_ref.shape[0]
         return (end + BATCH - 1) // BATCH
 
-    def pick(order, values):
-        return jnp.where(order == 0, values[0], jnp.where(order == 1, values[1], values[2]))
+    for i in range(6):
+        steps_z[i] = strides("z")[i]
+        steps_x[i] = strides("x")[i] * 2
 
     def panel(code):
-        block, order = (code >> 7) & 2047, (code >> 5) & 3
-        step_z, step_x = pick(order, strides("z")), pick(order, strides("x")) * 2
+        block, layout = (code >> 8) & 2047, (code >> 5) & 7
+        step_z, step_x = steps_z[layout], steps_x[layout]
         parts = [full[block + z * step_z + x_hi * step_x] for z in range(4) for x_hi in range(2)]
         return jnp.concatenate(parts, axis=0)
 
@@ -321,7 +355,7 @@
                 products = [
                     lax.dot_general(
                         panel(code),
-                        tiles[code >> 18],
+                        tiles[code >> 19],
                         (((1,), (1,)), ((), ())),
                         preferred_element_type=jnp.float32,
                     )
@@ -352,6 +386,8 @@
             pltpu.VMEM(early.shape, jnp.bfloat16),
             pltpu.VMEM((17, 256, TILE), jnp.float32),
             pltpu.SMEM((codes.size // 2 + BATCH + 8,), jnp.int32),
+            pltpu.SMEM((6,), jnp.int32),
+            pltpu.SMEM((6,), jnp.int32),
             pltpu.SemaphoreType.DMA((codes.shape[0],)),
         ],
         compiler_params=pltpu.CompilerParams(vmem_limit_bytes=17 * MIB),
@@ -405,17 +441,17 @@
         (((1,), (1,)), ((), ())),
         preferred_element_type=jnp.float32,
     )
-    terms[...] = local.reshape(terms.shape)
+    terms[...] = local.reshape(terms.shape).astype(terms.dtype)
     sent_terms = []
     for i in range(1, 8):
         to = (feat + i) % 8
         sent_terms.append(
             remote(terms.at[to], terms_in.at[i - 1], tsem.at[i - 1], tin.at[i - 1], {"feat": to})
         )
-    share = terms[feat]
+    share = terms[feat].astype(jnp.float32)
     for i in range(7):
         sent_terms[i].wait_recv()
-        share = share + terms_in[i]
+        share = share + terms_in[i].astype(jnp.float32)
     sums_ref[blk] = share.astype(sums_ref.dtype)
     sent_sums = []
     for i in range(1, 16):
@@ -444,8 +480,8 @@
         out_specs=(vmem, vmem),
         scratch_shapes=[
             pltpu.VMEM((7, 2, 256, TILE), jnp.bfloat16),
-            pltpu.VMEM((8, 32, 256), jnp.float32),
-            pltpu.VMEM((7, 32, 256), jnp.float32),
+            pltpu.VMEM((8, 32, 256), jnp.bfloat16),
+            pltpu.VMEM((7, 32, 256), jnp.bfloat16),
             dma((7,)), dma((7,)), dma((7,)), dma((7,)), dma((15,)), dma((15,)),
         ],
         compiler_params=pltpu.CompilerParams(collective_id=1, has_side_effects=True),

time: 93.6 us -> 90.9 us (0.971)
  Pallas kernels: 92.7 us -> 90 us
    pallas_call x1, Pallas kernels: 48.3 us -> 46.8 us  [gather(): pl.pallas_call(gather_kernel, out_shape=(pltpu.VMEM((2048, 32, TILE), jnp...]
    pallas_call x1, Pallas kernels: 38.2 us -> 37.1 us  [tail(): pl.pallas_call(tail_kernel, out_shape=(pltpu.VMEM((256, 256), jnp.bfloat1...]
where the time goes in v4:
time: 90.9 us; the launch traced here: 90.7 us
  Pallas kernels  90 us (99%)
    pallas_call x1, Pallas kernels, gather(): pl.pallas_call(gather_kernel, out_shape=(pltpu.VMEM((2048, 32, TILE), jnp...  46.8 us
    pallas_call x1, Pallas kernels, tail(): pl.pallas_call(tail_kernel, out_shape=(pltpu.VMEM((256, 256), jnp.bfloat1...  37.1 us
    pallas_call x1, Pallas kernels, aggregate(): pl.pallas_call(aggregate_kernel, out_shape=pltpu.VMEM((16, 256, TILE), jn...  5.49 us

profile of v4, /device:TPU:1, one launch (start us, length us, event | category | flops | bytes accessed | tf_op | source)
XLA Modules:
  0.0 90.7 jit_solution(5965275006225981805)
XLA Ops:
  0.6 0.0 copy-start
  0.6 46.8 %gather.1 = (bf16[2048,32,128]{2,1,0:T(8,128)(2,1)S(1)}, bf16[384,128,128]{2,1,0:T(8,128)(2,1)S(1)}, s32[16,48]{1,0:T(8,128)S(1)}) custom-call(bf16[32,2048]{1,0:T(8,128)(2,1)} %x_ref.1, bf16[768,128,128]{2,1,0:T(8,128)(2,1)} %bitcast.7, s32[16,48]{1,0:T(8,128)} %bitcast.9, s32[16,48]{1,0:T(8,128)} %bitcast.10), custom_call_target="tpu_custom_call" | custom-call | tf_op jit(solution)/shard_map/gather/pallas_call | solution.py:281
  47.4 0.0 copy-done
  47.4 5.5 %aggregate.1 = bf16[16,256,128]{2,1,0:T(8,128)(2,1)S(1)} custom-call(s32[16,48]{1,0:T(8,128)S(1)} %get-tuple-element.7.codes, s32[16]{0:T(128)S(1)} %bitcast.6, bf16[2048,32,128]{2,1,0:T(8,128)(2,1)S(1)} %get-tuple-element.8.full, bf16[384,128,128]{2,1,0:T(8,128)(2,1)S(1)} %get-tuple-element.9.early, bf16[768,128,128]{2,1,0:T(8,128)(2,1)} %bitcast.8), custom_call_target="tpu_custom_call" | custom-call | tf_op jit(solution)/shard_map/aggregate/pallas_call | solution.py:380
  52.9 37.1 %tail.1 = (bf16[256,256]{1,0:T(8,128)(2,1)S(1)}, bf16[16,32,256]{2,1,0:T(8,128)(2,1)S(1)}) custom-call(bf16[8,2,256,128]{3,2,1,0:T(8,128)(2,1)S(1)} %bitcast.5, bf16[256,256]{1,0:T(8,128)(2,1)} %weight.1, bf16[256,256]{1,0:T(8,128)(2,1)} %cotangent.1), custom_call_target="tpu_custom_call" | custom-call | tf_op jit(solution)/shard_map/tail/pallas_call | solution.py:473
  90.0 0.7 finish.1
Async XLA Ops:
  0.6 46.8 %copy-start = (s32[1,1,16]{2,1,0:T(1,128)S(1)}, s32[1,1,16]{2,1,0:T(1,128)}, u32[]{:S(2)}) copy-start(s32[1,1,16]{2,1,0:T(1,128)} %param.11) | copy-start | bytes 196

commit v5 on v4

--- a/solution.py
+++ b/solution.py
@@ -484,7 +484,9 @@
             pltpu.VMEM((7, 32, 256), jnp.bfloat16),
             dma((7,)), dma((7,)), dma((7,)), dma((7,)), dma((15,)), dma((15,)),
         ],
-        compiler_params=pltpu.CompilerParams(collective_id=1, has_side_effects=True),
+        compiler_params=pltpu.CompilerParams(
+            collective_id=1, has_side_effects=True, vmem_limit_bytes=10 * MIB
+        ),
         name="tail",
     )(in_vmem(part), weight, cotangent)
 

time: 90.9 us -> 90.6 us (level)
  no operation moved by 1% of the time
where the time goes in v5:
time: 90.6 us; the launch traced here: 90.9 us
  Pallas kernels  90.2 us (100%)
    pallas_call x1, Pallas kernels, gather(): pl.pallas_call(gather_kernel, out_shape=(pltpu.VMEM((2048, 32, TILE), jnp...  46.8 us
    pallas_call x1, Pallas kernels, tail(): pl.pallas_call(tail_kernel, out_shape=(pltpu.VMEM((256, 256), jnp.bfloat1...  36.4 us
    pallas_call x1, Pallas kernels, aggregate(): pl.pallas_call(aggregate_kernel, out_shape=pltpu.VMEM((16, 256, TILE), jn...  6.37 us

profile of v5, /device:TPU:1, one launch (start us, length us, event | category | flops | bytes accessed | tf_op | source)
XLA Modules:
  0.0 90.9 jit_solution(2945761512167079135)
XLA Ops:
  0.6 0.0 copy-start.2
  0.6 46.8 %gather.1 = (bf16[2048,32,128]{2,1,0:T(8,128)(2,1)S(1)}, bf16[384,128,128]{2,1,0:T(8,128)(2,1)S(1)}, s32[16,48]{1,0:T(8,128)S(1)}) custom-call(bf16[32,2048]{1,0:T(8,128)(2,1)} %x_ref.1, bf16[768,128,128]{2,1,0:T(8,128)(2,1)} %bitcast.7, s32[16,48]{1,0:T(8,128)} %bitcast.9, s32[16,48]{1,0:T(8,128)} %bitcast.10), custom_call_target="tpu_custom_call" | custom-call | tf_op jit(solution)/shard_map/gather/pallas_call | solution.py:281
  47.4 0.0 copy-done.2
  47.4 0.0 copy-start
  47.4 0.0 copy-start.1
  47.4 6.4 %aggregate.1 = bf16[16,256,128]{2,1,0:T(8,128)(2,1)S(1)} custom-call(s32[16,48]{1,0:T(8,128)S(1)} %get-tuple-element.7.codes, s32[16]{0:T(128)S(1)} %bitcast.6, bf16[2048,32,128]{2,1,0:T(8,128)(2,1)S(1)} %get-tuple-element.8.full, bf16[384,128,128]{2,1,0:T(8,128)(2,1)S(1)} %get-tuple-element.9.early, bf16[768,128,128]{2,1,0:T(8,128)(2,1)} %bitcast.8), custom_call_target="tpu_custom_call" | custom-call | tf_op jit(solution)/shard_map/aggregate/pallas_call | solution.py:380
  53.8 0.0 copy-done
  53.8 0.0 copy-done.1
  53.8 36.4 %tail.1 = (bf16[256,256]{1,0:T(8,128)(2,1)S(1)}, bf16[16,32,256]{2,1,0:T(8,128)(2,1)S(1)}) custom-call(bf16[8,2,256,128]{3,2,1,0:T(8,128)(2,1)S(1)} %bitcast.5, bf16[256,256]{1,0:T(8,128)(2,1)S(1)} %copy-done, bf16[256,256]{1,0:T(8,128)(2,1)S(1)} %copy-done.1), custom_call_target="tpu_custom_call" | custom-call | tf_op jit(solution)/shard_map/tail/pallas_call | solution.py:473
  90.3 0.7 finish.1
Async XLA Ops:
  0.6 46.8 %copy-start.2 = (s32[1,1,16]{2,1,0:T(1,128)S(1)}, s32[1,1,16]{2,1,0:T(1,128)}, u32[]{:S(2)}) copy-start(s32[1,1,16]{2,1,0:T(1,128)} %param.11) | copy-start | bytes 196
  47.4 6.4 %copy-start = (bf16[256,256]{1,0:T(8,128)(2,1)S(1)}, bf16[256,256]{1,0:T(8,128)(2,1)}, u32[]{:S(2)}) copy-start(bf16[256,256]{1,0:T(8,128)(2,1)} %weight.1) | copy-start | bytes 393220
  47.4 6.4 %copy-start.1 = (bf16[256,256]{1,0:T(8,128)(2,1)S(1)}, bf16[256,256]{1,0:T(8,128)(2,1)}, u32[]{:S(2)}) copy-start(bf16[256,256]{1,0:T(8,128)(2,1)} %cotangent.1) | copy-start | bytes 393220

commit v6 on v5

--- a/solution.py
+++ b/solution.py
@@ -419,14 +419,14 @@
         copy.start()
         return copy
 
-    sent = []
-    for i in range(1, 8):
+    sent = [None] * 7
+    for i in (5, 3, 4, 1, 7, 2, 6):
         to = (feat + i) % 8
-        sent.append(
-            remote(part.at[to], held.at[i - 1], psem.at[i - 1], pin.at[i - 1], {"feat": to})
+        sent[i - 1] = remote(
+            part.at[to], held.at[i - 1], psem.at[i - 1], pin.at[i - 1], {"feat": to}
         )
     summed = part[feat].astype(jnp.float32)
-    for i in range(7):
+    for i in (1, 5, 0, 6, 2, 3, 4):
         sent[i].wait_recv()
         summed = summed + held[i].astype(jnp.float32)
     nodes = summed.astype(jnp.bfloat16)

time: 90.6 us -> 91.2 us (level); the launches traced: 90.9 us -> 89.9 us
  Pallas kernels: 90.2 us -> 89.2 us
    pallas_call x1, Pallas kernels: 6.37 us -> 4.72 us  [aggregate(): pl.pallas_call(aggregate_kernel, out_shape=pltpu.VMEM((16, 256, TILE), jn...]
where the time goes in v6:
time: 91.2 us; the launch traced here: 89.9 us
  Pallas kernels  89.2 us (98%)
    pallas_call x1, Pallas kernels, gather(): pl.pallas_call(gather_kernel, out_shape=(pltpu.VMEM((2048, 32, TILE), jnp...  46.8 us
    pallas_call x1, Pallas kernels, tail(): pl.pallas_call(tail_kernel, out_shape=(pltpu.VMEM((256, 256), jnp.bfloat1...  37.1 us
    pallas_call x1, Pallas kernels, aggregate(): pl.pallas_call(aggregate_kernel, out_shape=pltpu.VMEM((16, 256, TILE), jn...  4.72 us

profile of v6, /device:TPU:1, one launch (start us, length us, event | category | flops | bytes accessed | tf_op | source)
XLA Modules:
  0.0 89.9 jit_solution(17956269229266964439)
XLA Ops:
  0.6 0.0 copy-start.2
  0.6 46.8 %gather.1 = (bf16[2048,32,128]{2,1,0:T(8,128)(2,1)S(1)}, bf16[384,128,128]{2,1,0:T(8,128)(2,1)S(1)}, s32[16,48]{1,0:T(8,128)S(1)}) custom-call(bf16[32,2048]{1,0:T(8,128)(2,1)} %x_ref.1, bf16[768,128,128]{2,1,0:T(8,128)(2,1)} %bitcast.7, s32[16,48]{1,0:T(8,128)} %bitcast.9, s32[16,48]{1,0:T(8,128)} %bitcast.10), custom_call_target="tpu_custom_call" | custom-call | tf_op jit(solution)/shard_map/gather/pallas_call | solution.py:281
  47.4 0.0 copy-done.2
  47.4 0.0 copy-start
  47.4 0.0 copy-start.1
  47.4 4.7 %aggregate.1 = bf16[16,256,128]{2,1,0:T(8,128)(2,1)S(1)} custom-call(s32[16,48]{1,0:T(8,128)S(1)} %get-tuple-element.7.codes, s32[16]{0:T(128)S(1)} %bitcast.6, bf16[2048,32,128]{2,1,0:T(8,128)(2,1)S(1)} %get-tuple-element.8.full, bf16[384,128,128]{2,1,0:T(8,128)(2,1)S(1)} %get-tuple-element.9.early, bf16[768,128,128]{2,1,0:T(8,128)(2,1)} %bitcast.8), custom_call_target="tpu_custom_call" | custom-call | tf_op jit(solution)/shard_map/aggregate/pallas_call | solution.py:380
  52.2 0.0 copy-done
  52.2 0.0 copy-done.1
  52.2 37.1 %tail.1 = (bf16[256,256]{1,0:T(8,128)(2,1)S(1)}, bf16[16,32,256]{2,1,0:T(8,128)(2,1)S(1)}) custom-call(bf16[8,2,256,128]{3,2,1,0:T(8,128)(2,1)S(1)} %bitcast.5, bf16[256,256]{1,0:T(8,128)(2,1)S(1)} %copy-done, bf16[256,256]{1,0:T(8,128)(2,1)S(1)} %copy-done.1), custom_call_target="tpu_custom_call" | custom-call | tf_op jit(solution)/shard_map/tail/pallas_call | solution.py:473
  89.3 0.7 finish.1
Async XLA Ops:
  0.6 46.8 %copy-start.2 = (s32[1,1,16]{2,1,0:T(1,128)S(1)}, s32[1,1,16]{2,1,0:T(1,128)}, u32[]{:S(2)}) copy-start(s32[1,1,16]{2,1,0:T(1,128)} %param.11) | copy-start | bytes 196
  47.4 4.8 %copy-start = (bf16[256,256]{1,0:T(8,128)(2,1)S(1)}, bf16[256,256]{1,0:T(8,128)(2,1)}, u32[]{:S(2)}) copy-start(bf16[256,256]{1,0:T(8,128)(2,1)} %weight.1) | copy-start | bytes 393220
  47.4 4.8 %copy-start.1 = (bf16[256,256]{1,0:T(8,128)(2,1)S(1)}, bf16[256,256]{1,0:T(8,128)(2,1)}, u32[]{:S(2)}) copy-start(bf16[256,256]{1,0:T(8,128)(2,1)} %cotangent.1) | copy-start | bytes 393220
